TPU v7x, 32 devices: a whole 2x2x4 slice. The times are simulated.
32 devices in a mesh: pair: 8 (over z, y), band: 4 (over x, core).
Axes of the slice: x: 2, y: 2, z: 4, core: 2. Of those that a mesh axis runs over, the one named last changes fastest.
Arguments:
- orbitals: bfloat16 [2048, 23, 64], P('pair'), may hold values from -6 to 6
- screening: bfloat16 [1024, 8, 1024], P('pair', None, 'band'), may hold values from -0.1875 to 0.1875
- trial: bfloat16 [1024, 23, 64], P('pair'), may hold values from -6 to 6
- pair_kpts: int32 [8, 2], replicated, may hold values from 0 to 22
- pair_q: int32 [8], replicated, may hold values from 0 to 7
Outputs:
- applied: float32 [1024, 23, 64], P('pair', None, 'band')
All inputs are finite; a program needn't handle non-finite values.
Results may differ from a plain program's by a relative error of at most 0.013.
Values may be sent and summed in bfloat16 or wider, within the bound.
No kernel may reach another device: no remote copies, remote signals or barrier semaphores. Data moves between devices by JAX's collectives and lax.ppermute only.
A program may use at most 64 MiB of HBM per device.

v0:
```python
import math
import jax
import jax.numpy as jnp
from jax import lax
from jax.sharding import PartitionSpec as P

NV = 32
NC = 32
NR = 2048
NG = 1024
KPTS = 23
NB = 64


def basis_rows(first_row, row_count, point_count):
    frequency = first_row + jnp.arange(row_count, dtype=jnp.int32)
    position = jnp.arange(point_count, dtype=jnp.int32)
    phase_index = (2 * position[None, :] + 1) * frequency[:, None] % (4 * point_count)
    values = jnp.cos(phase_index.astype(jnp.float32) * (math.pi / (2 * point_count))) * math.sqrt(
        2.0 / point_count
    )
    return values.astype(jnp.bfloat16)


def densities(first_set, second_set):
    merged = first_set.astype(jnp.float32)[:, :, None] * second_set.astype(jnp.float32)[:, None, :]
    return merged.reshape(first_set.shape[0], first_set.shape[1] * second_set.shape[1]).astype(
        jnp.bfloat16
    )


def transform(basis_block, first_set, second_set):
    return lax.dot_general(
        basis_block,
        densities(first_set, second_set),
        (((1,), (0,)), ((), ())),
        preferred_element_type=jnp.float32,
    ).astype(jnp.bfloat16)


def on_device(orbitals, screening, trial, pair_kpts, pair_q):
    band_count = lax.axis_size("band")
    pair_count = lax.axis_size("pair")
    pair_here = lax.axis_index("pair")
    own_kpts = lax.dynamic_index_in_dim(pair_kpts, pair_here, 0, keepdims=False)
    listed = pair_kpts.shape[0]
    vector_count = trial.shape[2]
    orbital_send = orbitals[:, pair_kpts].reshape(orbitals.shape[0], listed, 2 * NB)
    trial_send = trial[:, pair_kpts].reshape(trial.shape[0], listed, 2 * vector_count)
    screen_send = screening[:, pair_q]
    orbital_got, trial_got, screen_got = (
        lax.all_to_all(orbital_send, "pair", split_axis=1, concat_axis=0, tiled=True),
        lax.all_to_all(trial_send, "pair", split_axis=1, concat_axis=0, tiled=True),
        lax.all_to_all(screen_send, "pair", split_axis=1, concat_axis=0, tiled=True),
    )
    screen_cols = screen_got[:, 0]
    first_orb = orbital_got[:, 0, :NB]
    second_orb = orbital_got[:, 0, NB:]
    row_count = NG // band_count
    basis_block = basis_rows(lax.axis_index("band") * row_count, row_count, NR)
    valence = transform(basis_block, first_orb[:, :NV], second_orb[:, :NV])
    conduction = transform(basis_block, first_orb[:, NV:], second_orb[:, NV:])
    screened = lax.dot_general(
        screen_cols,
        lax.all_gather(valence, "band", axis=0, tiled=True),
        (((0,), (0,)), ((), ())),
        preferred_element_type=jnp.float32,
    ).astype(jnp.bfloat16)
    raw = lax.dot_general(
        conduction, screened, (((0,), (0,)), ((), ())), preferred_element_type=jnp.float32
    ) * (1.0 / math.sqrt(NG))
    kernel = (
        raw.reshape(NC, NC, NV, NV)
        .transpose(2, 0, 3, 1)
        .reshape(NV * NC, NV * NC)
        .astype(jnp.bfloat16)
    )
    trial_first = trial_got[:, 0, :vector_count]
    trial_second = trial_got[:, 0, vector_count:]
    apply_scale = 1.0 / math.sqrt(NV * NC)
    forward = (
        lax.dot_general(
            kernel, trial_second, (((1,), (0,)), ((), ())), preferred_element_type=jnp.float32
        )
        * apply_scale
    )
    backward = (
        lax.dot_general(
            kernel, trial_first, (((0,), (0,)), ((), ())), preferred_element_type=jnp.float32
        )
        * apply_scale
    )
    partials = jnp.stack([forward, backward])
    summed = lax.psum_scatter(
        partials.astype(jnp.bfloat16), "band", scatter_dimension=2, tiled=True
    ).astype(jnp.float32)
    share = summed.shape[2]
    state_rows = summed.shape[1] // pair_count
    kpt_ids = jnp.arange(KPTS, dtype=jnp.int32)
    one_hot = (own_kpts[:, None] == kpt_ids[None, :]).astype(jnp.float32)
    spread = (
        summed[0][:, None, :] * one_hot[0][None, :, None]
        + summed[1][:, None, :] * one_hot[1][None, :, None]
    )
    spread = spread.reshape(summed.shape[1], KPTS * share)
    scattered = lax.psum_scatter(spread, "pair", scatter_dimension=0, tiled=True)
    return scattered.reshape(state_rows, KPTS, share)


def solution(mesh):
    return jax.shard_map(
        on_device,
        mesh=mesh,
        in_specs=(P("pair", None, None), P("pair", None, "band"), P("pair", None, None), P(), P()),
        out_specs=P("pair", None, "band"),
        check_vma=False,
    )
```

profile of v0, /device:TPU:0, one launch (start us, length us, event | category | flops | bytes accessed | tf_op | source)
XLA Modules:
  0.0 212.1 jit_solution(7176523066295668518)
XLA Ops:
  6.5 0.8 compare_select_fusion
  7.3 0.1 copy.25
  7.4 0.1 reshape.56
  7.5 0.2 copy-done
  7.7 1.4 gather_fusion
  9.1 7.3 %all-to-all-start = ((bf16[256,8,128]{0,2,1:T(8,128)(2,1)}), bf16[256,8,128]{0,2,1:T(8,128)(2,1)S(1)}, u32[]{:S(2)}, u32[]{:S(2)}) async-start(bf16[256,8,128]{0,2,1:T(8,128)(2,1)} %bitcast.2), calls=%async_computation | async-start | bytes 1048576 | tf_op jit(solution)/shard_map/all_to_all | solution.py:52
  16.4 0.0 all-gather.2.cloned.1.call-start
  16.4 14.4 %all-to-all-done = bf16[256,8,128]{0,2,1:T(8,128)(2,1)S(1)} async-done(((bf16[256,8,128]{0,2,1:T(8,128)(2,1)}), bf16[256,8,128]{0,2,1:T(8,128)(2,1)S(1)}, u32[]{:S(2)}, u32[]{:S(2)}) %all-to-all-start) | async-done | bytes 524320 | tf_op jit(solution)/shard_map/all_to_all | solution.py:52
  30.9 0.3 copy.26
  31.1 0.2 fusion.23
  31.3 0.2 copy.28
  31.6 0.2 copy.27
  31.8 4.2 %multiply_convert_fusion = (bf16[2048,32,32]{0,2,1:T(8,128)(2,1)S(1)}, bf16[2048,32,32]{0,2,1:T(8,128)(2,1)}) fusion(f32[2048,32]{0,1:T(8,128)S(1)} %get-tuple-element.9, f32[2048,32]{0,1:T(8,128)S(1)} %get-tuple-element.7, f32[2048,32]{0,1:T(8,128)S(1)} %get-tuple-element.10, f32[2048,32]{0,1:T(8,128)S(1)} %get-tuple-element.8), kind=kLoop, calls=%fused_computation.3 | loop fusion | flops 8388608 | bytes 9437184 | tf_op jit(solution)/shard_map/convert_element_type | solution.py:27
  36.0 10.2 %convolution_convert_fusion.1 = bf16[256,1024]{1,0:T(8,128)(2,1)} fusion(bf16[2048,1024]{0,1:T(8,128)(2,1)S(1)} %bitcast.70, s32[256]{0:T(256)S(1)} %iota_add_fusion, s32[2048]{0:T(1024)S(1)} %multiply_add_fusion), kind=kOutput, calls=%fused_computation.21 | convolution fusion | flops 1082392576 | bytes 4727808 | tf_op jit(solution)/shard_map/dot_general | solution.py:33
  46.2 0.0 all-gather.2.cloned.1.call-update
  46.3 0.0 copy-done.2
  46.3 1.3 gather_fusion.2
  47.6 3.6 %all-to-all-start.2 = ((bf16[128,8,128]{0,2,1:T(8,128)(2,1)}), bf16[128,8,128]{0,2,1:T(8,128)(2,1)S(1)}, u32[]{:S(2)}, u32[]{:S(2)}) async-start(bf16[128,8,128]{0,2,1:T(8,128)(2,1)} %bitcast.17), calls=%async_computation.2 | async-start | bytes 524288 | tf_op jit(solution)/shard_map/all_to_all | solution.py:53
  51.3 0.0 copy-done.1
  51.3 2.0 gather_fusion.1
  53.3 0.9 copy.29
  54.2 6.1 %all-to-all-done.2 = bf16[128,8,128]{0,2,1:T(8,128)(2,1)S(1)} async-done(((bf16[128,8,128]{0,2,1:T(8,128)(2,1)}), bf16[128,8,128]{0,2,1:T(8,128)(2,1)S(1)}, u32[]{:S(2)}, u32[]{:S(2)}) %all-to-all-start.2) | async-done | bytes 262176 | tf_op jit(solution)/shard_map/all_to_all | solution.py:53
  60.3 3.6 %all-to-all-start.1 = ((bf16[128,8,256]{2,0,1:T(8,128)(2,1)}), bf16[128,8,256]{2,0,1:T(8,128)(2,1)S(1)}, u32[]{:S(2)}, u32[]{:S(2)}) async-start(bf16[128,8,256]{2,0,1:T(8,128)(2,1)} %copy.29), calls=%async_computation.1 | async-start | bytes 1048576 | tf_op jit(solution)/shard_map/all_to_all | solution.py:54
  63.9 0.2 reduce-scatter.3.cloned.1.call-start
  64.1 0.2 copy.31
  64.3 11.5 %convolution_convert_fusion.2 = bf16[256,1024]{1,0:T(8,128)(2,1)} fusion(bf16[2048,1024]{0,1:T(8,128)(2,1)} %bitcast.69, s32[256]{0:T(256)S(1)} %iota_add_fusion, s32[2048]{0:T(1024)S(1)} %multiply_add_fusion), kind=kOutput, calls=%fused_computation.22 | convolution fusion | flops 1082392576 | bytes 4727808 | tf_op jit(solution)/shard_map/dot_general | solution.py:33
  75.8 2.3 %all-to-all-done.1 = bf16[128,8,256]{2,0,1:T(8,128)(2,1)S(1)} async-done(((bf16[128,8,256]{2,0,1:T(8,128)(2,1)}), bf16[128,8,256]{2,0,1:T(8,128)(2,1)S(1)}, u32[]{:S(2)}, u32[]{:S(2)}) %all-to-all-start.1) | async-done | bytes 524320 | tf_op jit(solution)/shard_map/all_to_all | solution.py:54
  78.1 0.8 copy-done.3
  78.9 3.3 %multiply_convert_fusion.2 = bf16[1024,1024]{1,0:T(8,128)(2,1)S(1)} fusion(bf16[256,1024]{1,0:T(8,128)(2,1)} %convolution_convert_fusion.2, bf16[1024,256]{1,0:T(8,128)(2,1)} %bitcast.78, bf16[1024,1024]{1,0:T(8,128)(2,1)} %all-gather.2.cloned.1.call-done), kind=kOutput, calls=%fused_computation.5 | convolution fusion | flops 1076101120 | bytes 5242880 | tf_op jit(solution)/shard_map/dot_general | solution.py:69
  82.2 8.2 %convert_element_type.73 = bf16[32,32,32,32]{3,2,1,0:T(8,128)(2,1)} reshape(bf16[1024,1024]{1,0:T(8,128)(2,1)S(1)} %multiply_convert_fusion.2) | data formatting | bytes 4194304 | tf_op jit(solution)/shard_map/convert_element_type | solution.py:76
  90.4 15.2 %copy.30 = bf16[32,32,32,32]{1,3,0,2:T(8,128)(2,1)} copy(bf16[32,32,32,32]{3,2,1,0:T(8,128)(2,1)} %convert_element_type.73) | data formatting | bytes 4194304 | tf_op jit(solution)/shard_map/convert_element_type | solution.py:76
  105.6 11.3 %convert_element_type.75 = bf16[1024,1024]{1,0:T(8,128)(2,1)S(1)} reshape(bf16[32,32,32,32]{3,2,1,0:T(8,128)(2,1)} %bitcast.67) | data formatting | bytes 4194304 | tf_op jit(solution)/shard_map/convert_element_type | solution.py:76
  116.9 0.8 fusion.10
  117.8 0.5 fusion.9
  118.3 0.7 pad_maximum_fusion
  119.0 0.0 reduce-scatter.3.cloned.1.call-update
  119.0 0.0 reduce-scatter.5.cloned.1.call-start
  119.1 0.2 dynamic-slice_reduce_fusion
  119.3 0.1 compare_convert_fusion
  119.4 0.1 mul.153
  119.4 0.1 mul.154
  119.5 0.1 mul.161
  119.6 0.1 mul.162
  119.7 18.6 %reduce-scatter.3.cloned.1.call-done = bf16[2,1024,16]{1,2,0:T(8,128)(2,1)} async-done(((bf16[2,1024,64]{1,2,0:T(8,128)(2,1)}), bf16[2,1024,16]{1,2,0:T(8,128)(2,1)}) %reduce-scatter.3.cloned.1.call-update) | async-done | bytes 65552 | tf_op jit(solution)/shard_map/reduce_scatter | solution.py:94
  138.3 0.8 convert_element_type.76
  139.2 1.4 fusion.6
  140.5 0.0 reduce-scatter.5.cloned.1.call-update
  140.6 65.0 %reduce-scatter.5.cloned.1.call-done = f32[128,368]{0,1:T(8,128)} async-done(((f32[1024,368]{0,1:T(8,128)}), f32[128,368]{0,1:T(8,128)}) %reduce-scatter.5.cloned.1.call-update) | async-done | bytes 188432 | tf_op jit(solution)/shard_map/reduce_scatter | solution.py:106
  (18 shorter events, 0.1 us)
Async XLA Ops:
  6.5 1.1 copy-start
  9.1 21.8 %all-to-all-start = ((bf16[256,8,128]{0,2,1:T(8,128)(2,1)}), bf16[256,8,128]{0,2,1:T(8,128)(2,1)S(1)}, u32[]{:S(2)}, u32[]{:S(2)}) async-start(bf16[256,8,128]{0,2,1:T(8,128)(2,1)} %bitcast.2), calls=%async_computation | async-start | bytes 1048576 | tf_op jit(solution)/shard_map/all_to_all | solution.py:52
  16.4 61.8 %all-gather.2.cloned.1.call-start = ((), (), s32[]{:S(2)}) async-start(), calls=%async_computation.5 | async-start | bytes 2621440 | tf_op jit(solution)/shard_map/all_gather | solution.py:65
  36.0 10.2 %copy-start.2 = (bf16[128,23,64]{0,2,1:T(8,128)(2,1)S(1)}, bf16[128,23,64]{0,2,1:T(8,128)(2,1)}, u32[]{:S(2)}) copy-start(bf16[128,23,64]{0,2,1:T(8,128)(2,1)} %param.7) | copy-start | bytes 1130500
  46.2 5.0 %copy-start.5 = (s32[8]{0:T(128)S(1)}, s32[8]{0:T(128)}, u32[]{:S(2)}) copy-start(s32[8]{0:T(128)} %param.9) | copy-start | bytes 100
  46.2 5.0 %copy-start.1 = (bf16[128,8,256]{2,1,0:T(8,128)(2,1)S(1)}, bf16[128,8,256]{2,1,0:T(8,128)(2,1)}, u32[]{:S(2)}) copy-start(bf16[128,8,256]{2,1,0:T(8,128)(2,1)} %param.6) | copy-start | bytes 1572868
  47.6 12.7 %all-to-all-start.2 = ((bf16[128,8,128]{0,2,1:T(8,128)(2,1)}), bf16[128,8,128]{0,2,1:T(8,128)(2,1)S(1)}, u32[]{:S(2)}, u32[]{:S(2)}) async-start(bf16[128,8,128]{0,2,1:T(8,128)(2,1)} %bitcast.17), calls=%async_computation.2 | async-start | bytes 524288 | tf_op jit(solution)/shard_map/all_to_all | solution.py:53
  60.3 17.8 %all-to-all-start.1 = ((bf16[128,8,256]{2,0,1:T(8,128)(2,1)}), bf16[128,8,256]{2,0,1:T(8,128)(2,1)S(1)}, u32[]{:S(2)}, u32[]{:S(2)}) async-start(bf16[128,8,256]{2,0,1:T(8,128)(2,1)} %copy.29), calls=%async_computation.1 | async-start | bytes 1048576 | tf_op jit(solution)/shard_map/all_to_all | solution.py:54
  63.9 74.4 %reduce-scatter.3.cloned.1.call-start = ((), (), s32[]{:S(2)}) async-start(), calls=%async_computation.6 | async-start | bytes 327680 | tf_op jit(solution)/shard_map/reduce_scatter | solution.py:94
  78.1 0.8 copy-start.3
  117.7 1.3 copy-start.4
  119.0 86.5 %reduce-scatter.5.cloned.1.call-start = ((), (), s32[]{:S(2)}) async-start(), calls=%async_computation.7 | async-start | bytes 1695744 | tf_op jit(solution)/shard_map/reduce_scatter | solution.py:106
Sparse Core Ops, SparseCore 0:
  46.4 21.6 all-gather.1
  119.1 19.1 reduce-scatter.2
  141.7 63.7 reduce-scatter.4
where the time goes:
time: 213 us; the launch traced here: 212 us
  waiting for transfers between devices  106 us (50%)
  local copies, waits for them, and re-layouts  43.1 us (20%)
  matrix products  26.3 us (12%)
  starting transfers between devices  14.8 us (7%)
  between operations  13.3 us (6%)
  other arithmetic  8.09 us (4%)
    reduce_scatter x1, waiting for transfers between devices, on_device(): lax.psum_scatter(spread, 'pair', scatter_dimension=0, tiled=True)  65 us
    convert_element_type x3, local copies, waits for them, and re-layouts, on_device(): kernel = raw.reshape(NC, NC, NV, NV).transpose(2, 0, 3, 1).reshape(NV * N...  34.7 us
    dot_general x2, matrix products, transform(): lax.dot_general(basis_block, densities(first_set, second_set), (((1,), (0...  21.7 us
    reduce_scatter x1, waiting for transfers between devices, on_device(): lax.psum_scatter(partials.astype(jnp.bfloat16), 'band', scatter_dimension...  18.6 us
    all_to_all x1, waiting for transfers between devices, on_device(): lax.all_to_all(orbital_send, 'pair', split_axis=1, concat_axis=0, tiled=T...  14.4 us
    all_to_all x1, starting transfers between devices, on_device(): lax.all_to_all(orbital_send, 'pair', split_axis=1, concat_axis=0, tiled=T...  7.31 us
    all_to_all x1, waiting for transfers between devices, on_device(): lax.all_to_all(trial_send, 'pair', split_axis=1, concat_axis=0, tiled=True)  6.1 us
  transfers between devices with their start and end apart: 6, of which 5 were waited for; matrix products, arithmetic and copies ran while one was open for 8% of the time, Pallas kernels for 0%

commit v1 on v0

--- a/solution.py
+++ b/solution.py
@@ -1,3 +1,4 @@
+import functools
 import math
 import jax
 import jax.numpy as jnp
@@ -10,6 +11,27 @@
 NG = 1024
 KPTS = 23
 NB = 64
+
+
+def answer_units(work_x, mesh_ax):
+    r2 = jax.lax.axis_size(mesh_ax)
+    kept_arr = jax.lax.axis_index(mesh_ax)
+    mid_arr, s_next = (r2, kept_arr)
+    tmp = work_x.shape[1] // mid_arr
+    local_part = list(work_x.shape)
+    local_part[1] = tmp
+    top = local_part[0]
+    local_part[0] = top * mid_arr
+    part_now = jnp.zeros(local_part, work_x.dtype)
+    for w in range(mid_arr):
+        spare = lax.dynamic_slice_in_dim(work_x, (s_next ^ w) * tmp, tmp, axis=1)
+        if w:
+            spare = jax.lax.ppermute(spare, mesh_ax, [(k0, k0 ^ w) for k0 in range(mid_arr)])
+        part_now = lax.dynamic_update_slice_in_dim(part_now, spare, (s_next ^ w) * top, axis=0)
+    return part_now
+
+
+_wait_kinds = functools.partial(answer_units, mesh_ax="pair")
 
 
 def basis_rows(first_row, row_count, point_count):
@@ -49,7 +71,7 @@
     trial_send = trial[:, pair_kpts].reshape(trial.shape[0], listed, 2 * vector_count)
     screen_send = screening[:, pair_q]
     orbital_got, trial_got, screen_got = (
-        lax.all_to_all(orbital_send, "pair", split_axis=1, concat_axis=0, tiled=True),
+        _wait_kinds(orbital_send),
         lax.all_to_all(trial_send, "pair", split_axis=1, concat_axis=0, tiled=True),
         lax.all_to_all(screen_send, "pair", split_axis=1, concat_axis=0, tiled=True),
     )

time: 213 us -> 206 us (0.967)
  waiting for transfers between devices: 106 us -> 98.7 us
  starting transfers between devices: 14.8 us -> 20.4 us
    all_to_all x1 -> x0, waiting for transfers between devices: 14.4 us -> none  [on_device(): lax.all_to_all(orbital_send, 'pair', split_axis=1, concat_axis=0, tiled=T...]
    ppermute x0 -> x7, starting transfers between devices: none -> 12.6 us  [answer_units(): jax.lax.ppermute(spare, mesh_ax, [(k0, k0 ^ w) for k0 in range(mid_arr)])]
    all_to_all x1 -> x0, starting transfers between devices: 7.31 us -> none  [on_device(): lax.all_to_all(orbital_send, 'pair', split_axis=1, concat_axis=0, tiled=T...]
    ppermute x0 -> x7, waiting for transfers between devices: none -> 6.94 us  [answer_units(): jax.lax.ppermute(spare, mesh_ax, [(k0, k0 ^ w) for k0 in range(mid_arr)])]
  transfers between devices with their start and end apart: 6 -> 12, of which waited for: 5 -> 6; matrix products, arithmetic and copies ran while one was open for 8% -> 8% of each run, Pallas kernels for 0% -> 0%
where the time goes in v1:
time: 206 us; the launch traced here: 205 us
  waiting for transfers between devices  98.7 us (48%)
  local copies, waits for them, and re-layouts  41.3 us (20%)
  matrix products  25.1 us (12%)
  starting transfers between devices  20.4 us (10%)
  between operations  13.4 us (7%)
  other arithmetic  6.04 us (3%)
    reduce_scatter x1, waiting for transfers between devices, on_device(): lax.psum_scatter(spread, 'pair', scatter_dimension=0, tiled=True)  64.9 us
    convert_element_type x3, local copies, waits for them, and re-layouts, on_device(): kernel = raw.reshape(NC, NC, NV, NV).transpose(2, 0, 3, 1).reshape(NV * N...  34.5 us
    dot_general x2, matrix products, transform(): lax.dot_general(basis_block, densities(first_set, second_set), (((1,), (0...  20.4 us
    reduce_scatter x1, waiting for transfers between devices, on_device(): lax.psum_scatter(partials.astype(jnp.bfloat16), 'band', scatter_dimension...  18.7 us
    ppermute x7, starting transfers between devices, answer_units(): jax.lax.ppermute(spare, mesh_ax, [(k0, k0 ^ w) for k0 in range(mid_arr)])  12.6 us
    ppermute x7, waiting for transfers between devices, answer_units(): jax.lax.ppermute(spare, mesh_ax, [(k0, k0 ^ w) for k0 in range(mid_arr)])  6.94 us
    all_to_all x1, waiting for transfers between devices, on_device(): lax.all_to_all(trial_send, 'pair', split_axis=1, concat_axis=0, tiled=True)  5.69 us
  transfers between devices with their start and end apart: 12, of which 6 were waited for; matrix products, arithmetic and copies ran while one was open for 8% of the time, Pallas kernels for 0%

profile of v1, /device:TPU:0, one launch (start us, length us, event | category | flops | bytes accessed | tf_op | source)
XLA Modules:
  0.0 204.9 jit_solution(2601034642887058930)
XLA Ops:
  6.5 0.8 compare_select_fusion
  7.3 0.1 copy.19
  7.4 0.1 reshape.56
  7.5 0.2 copy-done
  7.7 0.6 gather_fusion
  8.3 0.1 constant_dynamic-slice_fusion.1
  8.4 3.1 %collective-permute-start = (bf16[256,1,128]{0,2,1:T(8,128)(2,1)S(1)}, bf16[256,1,128]{0,2,1:T(8,128)(2,1)S(1)}, u32[]{:S(2)}, u32[]{:S(2)}) collective-permute-start(bf16[256,1,128]{0,2,1:T(8,128)(2,1)S(1)} %get-tuple-element.13), channel_id=1, source_target_pairs={{0,4},{4,0},{8,12},{12,8},{16,20},{20,16},{24,28},{28,24},{1,5},{5... | collective-permute-start | bytes 196616 | tf_op jit(solution)/shard_map/ppermute | solution.py:29
  11.4 1.6 collective-permute-start.1
  13.0 3.0 %collective-permute-start.3 = (bf16[256,1,128]{0,2,1:T(8,128)(2,1)S(1)}, bf16[256,1,128]{0,2,1:T(8,128)(2,1)S(1)}, u32[]{:S(2)}, u32[]{:S(2)}) collective-permute-start(bf16[256,1,128]{0,2,1:T(8,128)(2,1)S(1)} %get-tuple-element.10), channel_id=1, source_target_pairs={{0,16},{4,20},{8,24},{12,28},{16,0},{20,4},{24,8},{28,12},{1,17},{... | collective-permute-start | bytes 196616 | tf_op jit(solution)/shard_map/ppermute | solution.py:29
  16.0 1.3 collective-permute-start.4
  17.3 3.7 %collective-permute-start.5 = (bf16[256,1,128]{0,2,1:T(8,128)(2,1)S(1)}, bf16[256,1,128]{0,2,1:T(8,128)(2,1)S(1)}, u32[]{:S(2)}, u32[]{:S(2)}) collective-permute-start(bf16[256,1,128]{0,2,1:T(8,128)(2,1)S(1)} %get-tuple-element.8), channel_id=1, source_target_pairs={{0,24},{4,28},{8,16},{12,20},{16,8},{20,12},{24,0},{28,4},{1,25},{... | collective-permute-start | bytes 196616 | tf_op jit(solution)/shard_map/ppermute | solution.py:29
  21.0 0.1 collective-permute-start.6
  21.2 5.1 %collective-permute-done.4 = bf16[256,1,128]{0,2,1:T(8,128)(2,1)S(1)} collective-permute-done((bf16[256,1,128]{0,2,1:T(8,128)(2,1)S(1)}, bf16[256,1,128]{0,2,1:T(8,128)(2,1)S(1)}, u32[]{:S(2)}, u32[]{:S(2)}) %collective-permute-start.4) | collective-permute-done | bytes 65568 | tf_op jit(solution)/shard_map/ppermute | solution.py:29
  26.2 1.9 collective-permute-done.6
  28.2 0.1 slice_convert_fusion
  28.3 1.1 multiply_convert_fusion
  29.4 10.2 %convolution_convert_fusion.1 = bf16[256,1024]{1,0:T(8,128)(2,1)} fusion(bf16[2048,1024]{0,1:T(8,128)(2,1)S(1)} %bitcast.68, s32[256]{0:T(256)S(1)} %iota_add_fusion, s32[2048]{0:T(1024)S(1)} %multiply_add_fusion), kind=kOutput, calls=%fused_computation.21 | convolution fusion | flops 1082392576 | bytes 4727808 | tf_op jit(solution)/shard_map/dot_general | solution.py:55
  39.6 0.0 all-gather.2.cloned.1.call-update
  39.6 1.3 gather_fusion.2
  40.9 3.9 %all-to-all-start.1 = ((bf16[128,8,128]{0,2,1:T(8,128)(2,1)}), bf16[128,8,128]{0,2,1:T(8,128)(2,1)S(1)}, u32[]{:S(2)}, u32[]{:S(2)}) async-start(bf16[128,8,128]{0,2,1:T(8,128)(2,1)} %bitcast.16), calls=%async_computation.1 | async-start | bytes 524288 | tf_op jit(solution)/shard_map/all_to_all | solution.py:75
  44.8 2.0 gather_fusion.1
  46.9 0.9 copy.20
  47.8 5.7 %all-to-all-done.1 = bf16[128,8,128]{0,2,1:T(8,128)(2,1)S(1)} async-done(((bf16[128,8,128]{0,2,1:T(8,128)(2,1)}), bf16[128,8,128]{0,2,1:T(8,128)(2,1)S(1)}, u32[]{:S(2)}, u32[]{:S(2)}) %all-to-all-start.1) | async-done | bytes 262176 | tf_op jit(solution)/shard_map/all_to_all | solution.py:75
  53.5 3.6 %all-to-all-start = ((bf16[128,8,256]{2,0,1:T(8,128)(2,1)}), bf16[128,8,256]{2,0,1:T(8,128)(2,1)S(1)}, u32[]{:S(2)}, u32[]{:S(2)}) async-start(bf16[128,8,256]{2,0,1:T(8,128)(2,1)} %copy.20), calls=%async_computation | async-start | bytes 1048576 | tf_op jit(solution)/shard_map/all_to_all | solution.py:76
  57.1 0.2 reduce-scatter.3.cloned.1.call-start
  57.3 1.1 multiply_convert_fusion.1
  58.4 10.2 %convolution_convert_fusion.2 = bf16[256,1024]{1,0:T(8,128)(2,1)} fusion(bf16[2048,1024]{0,1:T(8,128)(2,1)S(1)} %bitcast.67, s32[256]{0:T(256)S(1)} %iota_add_fusion, s32[2048]{0:T(1024)S(1)} %multiply_add_fusion), kind=kOutput, calls=%fused_computation.22 | convolution fusion | flops 1082392576 | bytes 4727808 | tf_op jit(solution)/shard_map/dot_general | solution.py:55
  68.6 0.2 copy.22
  68.8 2.5 %all-to-all-done = bf16[128,8,256]{2,0,1:T(8,128)(2,1)S(1)} async-done(((bf16[128,8,256]{2,0,1:T(8,128)(2,1)}), bf16[128,8,256]{2,0,1:T(8,128)(2,1)S(1)}, u32[]{:S(2)}, u32[]{:S(2)}) %all-to-all-start) | async-done | bytes 524320 | tf_op jit(solution)/shard_map/all_to_all | solution.py:76
  71.2 0.8 copy-done.3
  72.0 3.3 %multiply_convert_fusion.2 = bf16[1024,1024]{1,0:T(8,128)(2,1)S(1)} fusion(bf16[256,1024]{1,0:T(8,128)(2,1)} %convolution_convert_fusion.2, bf16[1024,256]{1,0:T(8,128)(2,1)} %bitcast.73, bf16[1024,1024]{1,0:T(8,128)(2,1)} %all-gather.2.cloned.1.call-done), kind=kOutput, calls=%fused_computation.5 | convolution fusion | flops 1076101120 | bytes 5242880 | tf_op jit(solution)/shard_map/dot_general | solution.py:91
  75.3 7.9 %convert_element_type.73 = bf16[32,32,32,32]{3,2,1,0:T(8,128)(2,1)} reshape(bf16[1024,1024]{1,0:T(8,128)(2,1)S(1)} %multiply_convert_fusion.2) | data formatting | bytes 4194304 | tf_op jit(solution)/shard_map/convert_element_type | solution.py:98
  83.3 15.2 %copy.21 = bf16[32,32,32,32]{1,3,0,2:T(8,128)(2,1)} copy(bf16[32,32,32,32]{3,2,1,0:T(8,128)(2,1)} %convert_element_type.73) | data formatting | bytes 4194304 | tf_op jit(solution)/shard_map/convert_element_type | solution.py:98
  98.5 11.3 %convert_element_type.75 = bf16[1024,1024]{1,0:T(8,128)(2,1)S(1)} reshape(bf16[32,32,32,32]{3,2,1,0:T(8,128)(2,1)} %bitcast.65) | data formatting | bytes 4194304 | tf_op jit(solution)/shard_map/convert_element_type | solution.py:98
  109.8 0.8 fusion.10
  110.6 0.5 fusion.9
  111.1 0.7 pad_maximum_fusion
  111.9 0.0 reduce-scatter.5.cloned.1.call-start
  112.0 0.2 fusion.15
  112.1 0.1 compare_convert_fusion
  112.2 0.1 mul.185
  112.3 0.1 mul.186
  112.4 0.1 mul.193
  112.4 0.1 mul.194
  112.5 18.7 %reduce-scatter.3.cloned.1.call-done = bf16[2,1024,16]{1,2,0:T(8,128)(2,1)} async-done(((bf16[2,1024,64]{1,2,0:T(8,128)(2,1)}), bf16[2,1024,16]{1,2,0:T(8,128)(2,1)}) %reduce-scatter.3.cloned.1.call-update) | async-done | bytes 65552 | tf_op jit(solution)/shard_map/reduce_scatter | solution.py:116
  131.2 0.8 convert_element_type.76
  132.1 1.4 fusion.6
  133.5 64.9 %reduce-scatter.5.cloned.1.call-done = f32[128,368]{0,1:T(8,128)} async-done(((f32[1024,368]{0,1:T(8,128)}), f32[128,368]{0,1:T(8,128)}) %reduce-scatter.5.cloned.1.call-update) | async-done | bytes 188432 | tf_op jit(solution)/shard_map/reduce_scatter | solution.py:128
  (36 shorter events, 0.3 us)
Async XLA Ops:
  6.5 1.1 copy-start
  6.5 64.7 %all-gather.2.cloned.1.call-start = ((), (), s32[]{:S(2)}) async-start(), calls=%async_computation.4 | async-start | bytes 2621440 | tf_op jit(solution)/shard_map/all_gather | solution.py:87
  8.4 8.9 %collective-permute-start = (bf16[256,1,128]{0,2,1:T(8,128)(2,1)S(1)}, bf16[256,1,128]{0,2,1:T(8,128)(2,1)S(1)}, u32[]{:S(2)}, u32[]{:S(2)}) collective-permute-start(bf16[256,1,128]{0,2,1:T(8,128)(2,1)S(1)} %get-tuple-element.13), channel_id=1, source_target_pairs={{0,4},{4,0},{8,12},{12,8},{16,20},{20,16},{24,28},{28,24},{1,5},{5... | collective-permute-start | bytes 196616 | tf_op jit(solution)/shard_map/ppermute | solution.py:29
  11.4 9.5 %collective-permute-start.1 = (bf16[256,1,128]{0,2,1:T(8,128)(2,1)S(1)}, bf16[256,1,128]{0,2,1:T(8,128)(2,1)S(1)}, u32[]{:S(2)}, u32[]{:S(2)}) collective-permute-start(bf16[256,1,128]{0,2,1:T(8,128)(2,1)S(1)} %get-tuple-element.12), channel_id=1, source_target_pairs={{0,8},{4,12},{8,0},{12,4},{16,24},{20,28},{24,16},{28,20},{1,9},{5... | collective-permute-start | bytes 196616 | tf_op jit(solution)/shard_map/ppermute | solution.py:29
  13.0 8.1 %collective-permute-start.2 = (bf16[256,1,128]{0,2,1:T(8,128)(2,1)S(1)}, bf16[256,1,128]{0,2,1:T(8,128)(2,1)S(1)}, u32[]{:S(2)}, u32[]{:S(2)}) collective-permute-start(bf16[256,1,128]{0,2,1:T(8,128)(2,1)S(1)} %get-tuple-element.11), channel_id=1, source_target_pairs={{0,12},{4,8},{8,4},{12,0},{16,28},{20,24},{24,20},{28,16},{1,13},{... | collective-permute-start | bytes 196616 | tf_op jit(solution)/shard_map/ppermute | solution.py:29
  13.0 8.1 %collective-permute-start.3 = (bf16[256,1,128]{0,2,1:T(8,128)(2,1)S(1)}, bf16[256,1,128]{0,2,1:T(8,128)(2,1)S(1)}, u32[]{:S(2)}, u32[]{:S(2)}) collective-permute-start(bf16[256,1,128]{0,2,1:T(8,128)(2,1)S(1)} %get-tuple-element.10), channel_id=1, source_target_pairs={{0,16},{4,20},{8,24},{12,28},{16,0},{20,4},{24,8},{28,12},{1,17},{... | collective-permute-start | bytes 196616 | tf_op jit(solution)/shard_map/ppermute | solution.py:29
  16.0 10.2 %collective-permute-start.4 = (bf16[256,1,128]{0,2,1:T(8,128)(2,1)S(1)}, bf16[256,1,128]{0,2,1:T(8,128)(2,1)S(1)}, u32[]{:S(2)}, u32[]{:S(2)}) collective-permute-start(bf16[256,1,128]{0,2,1:T(8,128)(2,1)S(1)} %get-tuple-element.9), channel_id=1, source_target_pairs={{0,20},{4,16},{8,28},{12,24},{16,4},{20,0},{24,12},{28,8},{1,21},{... | collective-permute-start | bytes 196616 | tf_op jit(solution)/shard_map/ppermute | solution.py:29
  17.3 8.9 %collective-permute-start.5 = (bf16[256,1,128]{0,2,1:T(8,128)(2,1)S(1)}, bf16[256,1,128]{0,2,1:T(8,128)(2,1)S(1)}, u32[]{:S(2)}, u32[]{:S(2)}) collective-permute-start(bf16[256,1,128]{0,2,1:T(8,128)(2,1)S(1)} %get-tuple-element.8), channel_id=1, source_target_pairs={{0,24},{4,28},{8,16},{12,20},{16,8},{20,12},{24,0},{28,4},{1,25},{... | collective-permute-start | bytes 196616 | tf_op jit(solution)/shard_map/ppermute | solution.py:29
  21.0 7.1 %collective-permute-start.6 = (bf16[256,1,128]{0,2,1:T(8,128)(2,1)S(1)}, bf16[256,1,128]{0,2,1:T(8,128)(2,1)S(1)}, u32[]{:S(2)}, u32[]{:S(2)}) collective-permute-start(bf16[256,1,128]{0,2,1:T(8,128)(2,1)S(1)} %get-tuple-element.7), channel_id=1, source_target_pairs={{0,28},{4,24},{8,20},{12,16},{16,12},{20,8},{24,4},{28,0},{1,29},{... | collective-permute-start | bytes 196616 | tf_op jit(solution)/shard_map/ppermute | solution.py:29
  29.3 10.3 %copy-start.2 = (bf16[128,23,64]{0,2,1:T(8,128)(2,1)S(1)}, bf16[128,23,64]{0,2,1:T(8,128)(2,1)}, u32[]{:S(2)}) copy-start(bf16[128,23,64]{0,2,1:T(8,128)(2,1)} %param.7) | copy-start | bytes 1130500
  39.6 5.2 %copy-start.5 = (s32[8]{0:T(128)S(1)}, s32[8]{0:T(128)}, u32[]{:S(2)}) copy-start(s32[8]{0:T(128)} %param.9) | copy-start | bytes 100
  39.6 5.3 %copy-start.1 = (bf16[128,8,256]{2,1,0:T(8,128)(2,1)S(1)}, bf16[128,8,256]{2,1,0:T(8,128)(2,1)}, u32[]{:S(2)}) copy-start(bf16[128,8,256]{2,1,0:T(8,128)(2,1)} %param.6) | copy-start | bytes 1572868
  40.9 12.6 %all-to-all-start.1 = ((bf16[128,8,128]{0,2,1:T(8,128)(2,1)}), bf16[128,8,128]{0,2,1:T(8,128)(2,1)S(1)}, u32[]{:S(2)}, u32[]{:S(2)}) async-start(bf16[128,8,128]{0,2,1:T(8,128)(2,1)} %bitcast.16), calls=%async_computation.1 | async-start | bytes 524288 | tf_op jit(solution)/shard_map/all_to_all | solution.py:75
  53.5 17.8 %all-to-all-start = ((bf16[128,8,256]{2,0,1:T(8,128)(2,1)}), bf16[128,8,256]{2,0,1:T(8,128)(2,1)S(1)}, u32[]{:S(2)}, u32[]{:S(2)}) async-start(bf16[128,8,256]{2,0,1:T(8,128)(2,1)} %copy.20), calls=%async_computation | async-start | bytes 1048576 | tf_op jit(solution)/shard_map/all_to_all | solution.py:76
  57.1 74.1 %reduce-scatter.3.cloned.1.call-start = ((), (), s32[]{:S(2)}) async-start(), calls=%async_computation.5 | async-start | bytes 327680 | tf_op jit(solution)/shard_map/reduce_scatter | solution.py:116
  71.2 0.8 copy-start.3
  110.6 1.3 copy-start.4
  111.9 86.5 %reduce-scatter.5.cloned.1.call-start = ((), (), s32[]{:S(2)}) async-start(), calls=%async_computation.6 | async-start | bytes 1695744 | tf_op jit(solution)/shard_map/reduce_scatter | solution.py:128
Sparse Core Ops, SparseCore 0:
  39.7 21.8 all-gather.1
  112.0 19.1 reduce-scatter.2
  134.6 63.6 reduce-scatter.4
